TPU v7x, 256 devices: a whole 4x4x8 slice. The times are simulated.
256 devices in a mesh: dp: 2 (over z_lo), seq: 32 (over y, x, core), head: 4 (over z_hi).
Axes of the slice: x: 4, y: 4, z: 8 (z_hi: 4, z_lo: 2; z = z_hi * 2 + z_lo), core: 2. Of those that a mesh axis runs over, the one named last changes fastest.
Arguments:
- query_rows: bfloat16 [2, 8192, 4096], P('dp', 'seq', 'head'), may hold values from -0.59765625 to 0.59765625
- key_rows: bfloat16 [2, 8192, 4096], P('dp', 'seq', 'head'), may hold values from -0.59765625 to 0.59765625
- value_rows: bfloat16 [2, 8192, 4096], P('dp', 'seq', 'head'), may hold values from -1536 to 1536
- grad_out: bfloat16 [2, 8192, 6144], P('dp', 'seq'), may hold values from -6 to 6
- out_weight: bfloat16 [6144, 4096], P('seq', 'head'), may hold values from -0.09375 to 0.09375
- decay_rates: float32 [32], P('head'), may hold values from 0 to 1, as said below
- doc_blocks: int32 [2, 64], P('dp'), may hold values from 0 to 7, never falling along the last dimension, each value on 1 to 32 neighbouring positions
Outputs:
- grad_query: bfloat16 [2, 8192, 4096], P('dp', 'seq', 'head')
- grad_key: bfloat16 [2, 8192, 4096], P('dp', 'seq', 'head')
- grad_value: bfloat16 [2, 8192, 4096], P('dp', 'seq', 'head')
- grad_weight: float32 [6144, 4096], P('seq', 'head')
Inputs may be any that keep to these rules, and one draw needn't show every extreme that they name: `doc_blocks`: in each pack document numbers never fall from block to block; every document covers 1 to 32 blocks, and one covers exactly 32. `decay_rates`: rates are positive.
All inputs are finite; a program needn't handle non-finite values.
Results may differ from a plain program's by a relative error of at most 0.024.
Values may be sent and summed in bfloat16 or wider, within the bound.
No kernel may reach another device: no remote copies, remote signals or barrier semaphores. Data moves between devices by JAX's collectives and lax.ppermute only.
A program may use at most 192 MiB of HBM per device.

v0:
```python
import jax
import jax.numpy as jnp
from jax import lax
from jax.sharding import PartitionSpec as P

BLOCK = 128
EPSILON = 1e-05


def prefix(array, axis, join, neutral, backward):
    count = lax.axis_size(axis)
    place = lax.axis_index(axis)
    ahead = count - 1 - place if backward else place
    gathered = jax.tree.map(
        lambda a, kind: lax.all_gather(a.astype(kind), axis), array, (jnp.bfloat16, jnp.bfloat16)
    )
    state = jax.tree.map(lambda a, e: jnp.zeros_like(a) + jnp.asarray(e, a.dtype), array, neutral)

    def one(step, state):
        source = count - 1 - step if backward else step
        return join(
            state,
            jax.tree.map(
                lambda a, own: lax.dynamic_index_in_dim(a, source, 0, False).astype(own.dtype),
                gathered,
                array,
            ),
        )

    return lax.fori_loop(0, ahead, one, state)


def block_docs(doc_row, first_block, block_count, block_len):
    blocks = lax.dynamic_slice_in_dim(doc_row, first_block, block_count)
    return jnp.reshape(
        jnp.broadcast_to(blocks[:, None], (block_count, block_len)), (block_count * block_len,)
    )


def decay_masks(token_docs, decay_rates, prev_doc, next_doc):
    length = token_docs.shape[0]
    position = jnp.arange(length).astype(jnp.float32)
    rates = decay_rates[:, None]
    distance = position[:, None] - position[None, :]
    allowed = jnp.logical_and(distance >= 0, token_docs[:, None] == token_docs[None, :])
    intra = jnp.where(
        allowed[None], jnp.exp(-rates[:, :, None] * jnp.maximum(distance, 0.0)[None]), 0.0
    )
    weight_end = jnp.where(
        (token_docs == token_docs[length - 1])[None],
        jnp.exp(-rates * (length - 1.0 - position)[None]),
        0.0,
    )
    weight_start = jnp.where(
        (token_docs == token_docs[0])[None], jnp.exp(-rates * position[None]), 0.0
    )
    weight_before = jnp.where(
        (token_docs == prev_doc)[None], jnp.exp(-rates * (position + 1.0)[None]), 0.0
    )
    weight_after = jnp.where(
        (token_docs == next_doc)[None], jnp.exp(-rates * (length - position)[None]), 0.0
    )
    span_decay = jnp.exp(-decay_rates * float(length))
    link_fwd = jnp.where(token_docs[length - 1] == prev_doc, span_decay, 0.0)
    link_rev = jnp.where(token_docs[0] == next_doc, span_decay, 0.0)
    return (intra, weight_end, weight_start, weight_before, weight_after, link_fwd, link_rev)


def combine_states(earlier, later):
    return (earlier[0] * later[0], later[0][:, None, None] * earlier[1] + later[1])


def local_state(keys_here, values_here, weight_end):
    weighted = (keys_here.astype(jnp.float32) * weight_end.T[:, :, None]).astype(jnp.bfloat16)
    return jnp.einsum("jhd,jhe->hde", weighted, values_here, preferred_element_type=jnp.float32)


def forward_out(queries, keys_here, values_here, intra, weight_before, state_in):
    scores = jnp.einsum("thd,jhd->htj", queries, keys_here, preferred_element_type=jnp.float32)
    attention = (scores * intra).astype(jnp.bfloat16)
    state_low = state_in.astype(jnp.bfloat16)
    carried = jnp.einsum("thd,hde->the", queries, state_low, preferred_element_type=jnp.float32)
    output = (
        jnp.einsum("htj,jhe->the", attention, values_here, preferred_element_type=jnp.float32)
        + weight_before.T[:, :, None] * carried
    )
    inverse_rms = lax.rsqrt(jnp.mean(output * output, axis=-1, keepdims=True) + EPSILON)
    return (attention, state_low, output * inverse_rms, inverse_rms)


def backward_local(queries, values_here, intra, normal, inverse_rms, grad_normed, weight_start):
    inner = jnp.mean(grad_normed * normal, axis=-1, keepdims=True)
    grad_attn = (inverse_rms * (grad_normed - normal * inner)).astype(jnp.bfloat16)
    grad_scores = (
        jnp.einsum("the,jhe->htj", grad_attn, values_here, preferred_element_type=jnp.float32)
        * intra
    ).astype(jnp.bfloat16)
    weighted = (queries.astype(jnp.float32) * weight_start.T[:, :, None]).astype(jnp.bfloat16)
    back_local = jnp.einsum("thd,the->hde", weighted, grad_attn, preferred_element_type=jnp.float32)
    return (grad_attn, grad_scores, back_local)


def backward_rest(
    queries,
    keys_here,
    values_here,
    attention,
    state_low,
    grad_attn,
    grad_scores,
    weight_before,
    weight_after,
    state_back,
):
    back_low = state_back.astype(jnp.bfloat16)
    grad_query = jnp.einsum(
        "htj,jhd->thd", grad_scores, keys_here, preferred_element_type=jnp.float32
    ) + weight_before.T[:, :, None] * jnp.einsum(
        "the,hde->thd", grad_attn, state_low, preferred_element_type=jnp.float32
    )
    grad_key = jnp.einsum(
        "htj,thd->jhd", grad_scores, queries, preferred_element_type=jnp.float32
    ) + weight_after.T[:, :, None] * jnp.einsum(
        "jhe,hde->jhd", values_here, back_low, preferred_element_type=jnp.float32
    )
    grad_value = jnp.einsum(
        "htj,the->jhe", attention, grad_attn, preferred_element_type=jnp.float32
    ) + weight_after.T[:, :, None] * jnp.einsum(
        "jhd,hde->jhe", keys_here, back_low, preferred_element_type=jnp.float32
    )
    return (
        grad_query.astype(jnp.bfloat16),
        grad_key.astype(jnp.bfloat16),
        grad_value.astype(jnp.bfloat16),
    )


def local(query_rows, key_rows, value_rows, grad_out, out_weight, decay_rates, doc_blocks):
    tok_count = query_rows.shape[1]
    heads_here = decay_rates.shape[0]
    head_dim = query_rows.shape[2] // heads_here
    seq_count = lax.axis_size("seq")
    span_index = lax.axis_index("seq")
    block_count = tok_count // BLOCK
    total_blocks = doc_blocks.shape[1]
    queries = query_rows[0].reshape(tok_count, heads_here, head_dim)
    keys_here = key_rows[0].reshape(tok_count, heads_here, head_dim)
    values_here = value_rows[0].reshape(tok_count, heads_here, head_dim)
    grad_rows = grad_out[0]
    doc_row = doc_blocks[0]
    first_block = span_index * block_count
    token_docs = block_docs(doc_row, first_block, block_count, BLOCK)
    prev_doc = doc_row[jnp.maximum(first_block - 1, 0)]
    next_doc = doc_row[jnp.minimum(first_block + block_count, total_blocks - 1)]
    intra, weight_end, weight_start, weight_before, weight_after, link_fwd, link_rev = decay_masks(
        token_docs, decay_rates, prev_doc, next_doc
    )
    state_local = local_state(keys_here, values_here, weight_end)
    identity = (jnp.ones_like(link_fwd), jnp.zeros_like(state_local))
    state_in = prefix((link_fwd, state_local), "seq", combine_states, identity, False)[1]
    attention, state_low, normal, inverse_rms = forward_out(
        queries, keys_here, values_here, intra, weight_before, state_in
    )
    columns = grad_rows
    grad_normed = jnp.dot(
        columns,
        lax.all_gather(out_weight, "seq", axis=0, tiled=True),
        preferred_element_type=jnp.float32,
    )
    normed = normal.astype(jnp.bfloat16).reshape(tok_count, heads_here * head_dim)
    columns = grad_rows
    part = lax.dot_general(
        columns, normed, (((0,), (0,)), ((), ())), preferred_element_type=jnp.float32
    )
    weight_part = lax.psum_scatter(
        part.astype(jnp.bfloat16).astype(jnp.float32).astype(jnp.bfloat16),
        "seq",
        scatter_dimension=0,
        tiled=True,
    )
    norm_factor = (lax.axis_size("dp") * seq_count * tok_count) ** (-0.5)
    grad_weight = lax.psum(weight_part, "dp").astype(jnp.float32) * norm_factor
    grad_attn, grad_scores, back_local = backward_local(
        queries,
        values_here,
        intra,
        normal,
        inverse_rms,
        grad_normed.reshape(tok_count, heads_here, head_dim),
        weight_start,
    )
    back_identity = (jnp.ones_like(link_rev), jnp.zeros_like(back_local))
    state_back = prefix((link_rev, back_local), "seq", combine_states, back_identity, True)[1]
    grad_query, grad_key, grad_value = backward_rest(
        queries,
        keys_here,
        values_here,
        attention,
        state_low,
        grad_attn,
        grad_scores,
        weight_before,
        weight_after,
        state_back,
    )
    flat_shape = (1, tok_count, heads_here * head_dim)
    return (
        grad_query.reshape(flat_shape),
        grad_key.reshape(flat_shape),
        grad_value.reshape(flat_shape),
        grad_weight,
    )


def solution(mesh):
    in_specs = (
        P("dp", "seq", "head"),
        P("dp", "seq", "head"),
        P("dp", "seq", "head"),
        P("dp", "seq", None),
        P("seq", "head"),
        P("head"),
        P("dp", None),
    )
    out_specs = (
        P("dp", "seq", "head"),
        P("dp", "seq", "head"),
        P("dp", "seq", "head"),
        P("seq", "head"),
    )
    return jax.shard_map(local, mesh=mesh, in_specs=in_specs, out_specs=out_specs, check_vma=False)
```

profile of v0, /device:TPU:1, one launch (start us, length us, event | category | flops | bytes accessed | tf_op | source)
XLA Modules:
  0.0 419.0 jit_solution(4983138501228653416)
XLA Ops:
  12.7 2.7 bitcast_compare_fusion.3
  15.4 1.9 copy.85
  17.3 2.1 copy.58
  21.4 2.0 convolution_convert_fusion.1
  26.0 66.1 %all-reduce.2 = (bf16[256]{0:T(256)(128)(2,1)S(1)}, bf16[256]{0:T(256)(128)(2,1)S(1)}) all-reduce(bf16[256]{0:T(256)(128)(2,1)S(1)} %dynamic-update-slice, bf16[256]{0:T(256)(128)(2,1)S(1)} %dynamic-update-slice.1), channel_id=2, replica_groups=mesh['dp'=2,'seq'=32,'head'=4] {'seq'}, use_global_device_ids=true, to_apply=%add | all-reduce | flops 512 | bytes 2048
  92.1 2.1 copy.84
  99.7 2.1 while.26
  99.7 2.1 convert_add_fusion.4
  101.8 3.0 multiply_reduce_fusion.1
  104.7 51.4 %all-gather.8.cloned.1.call-done = bf16[6144,1024]{1,0:T(8,128)(2,1)} async-done(((bf16[192,1024]{1,0:T(8,128)(2,1)}), bf16[6144,1024]{1,0:T(8,128)(2,1)}) %all-gather.8.cloned.1.call-update) | async-done | bytes 12582928 | tf_op jit(solution)/shard_map/all_gather | solution.py:167
  156.1 16.7 %copy.62 = bf16[1024,6144]{1,0:T(8,128)(2,1)} copy(bf16[1024,6144]{0,1:T(8,128)(2,1)} %bitcast.111) | data formatting | bytes 25165824 | tf_op jit(solution)/shard_map/dot_general | solution.py:165
  172.8 7.0 %multiply_reduce_fusion = (f32[256,8]{0,1:T(8,128)S(1)}, f32[256,8,128]{0,2,1:T(8,128)S(1)}) fusion(f32[256,8,128]{0,2,1:T(8,128)} %get-tuple-element.186, f32[256,8]{0,1:T(8,128)S(1)} %add_rsqrt_fusion, bf16[8,128,6144]{2,1,0:T(8,128)(2,1)} %bitcast.112, bf16[1,256,6144]{2,1,0:T(8,128)(2,1)S(1)} %copy-done), kind=kOutput, calls=%fused_computation.35 | convolution fusion | flops 3222009856 | bytes 17842176 | tf_op jit(solution)/shard_map/dot_general | solution.py:165
  182.8 7.4 %convert_bitcast_fusion = bf16[6144,1024]{0,1:T(8,128)(2,1)} fusion(bf16[256,1024]{0,1:T(8,128)(2,1)} %bitcast.127, bf16[1,256,6144]{2,1,0:T(8,128)(2,1)S(1)} %copy-done), kind=kOutput, calls=%fused_computation.4 | convolution fusion | flops 3227516928 | bytes 16252928 | tf_op jit(solution)/shard_map/dot_general | solution.py:172
  190.2 16.7 %copy.82 = bf16[6144,1024]{1,0:T(8,128)(2,1)} copy(bf16[6144,1024]{0,1:T(8,128)(2,1)} %convert_bitcast_fusion) | data formatting | bytes 25165824
  213.4 37.4 %all-gather.12.cloned.1.call-done = bf16[256,128,128]{2,1,0:T(8,128)(2,1)} async-done(((bf16[8,128,128]{2,1,0:T(8,128)(2,1)}), bf16[256,128,128]{2,1,0:T(8,128)(2,1)}) %all-gather.12.cloned.1.call-update) | async-done | bytes 8388624 | tf_op jit(solution)/shard_map/all_gather | solution.py:15
  250.9 35.0 %while.27 = (s32[]{:T(128)}, f32[8,128,128]{2,1,0:T(8,128)S(1)}, s32[]{:T(128)}, bf16[32,8]{1,0:T(8,128)(2,1)S(1)}, bf16[32,8,128,128]{3,2,1,0:T(8,128)(2,1)}, /*index=5*/s32[]{:T(128)}, s32[]{:T(128)}, s32[]{:T(128)}, s32[]{:T(128)}) while((s32[]{:T(128)}, f32[8,128,128]{2,1,0:T(8,128)S(1)}, s32[]{:T(128)}, bf16[32,8]{1,0:T(8,128)(2,1)S(1)}, ...), condition=%wide.region_5.6_spmd, body=%wide.region_4.5_spmd.sunk | while | flops 393230 | bytes 1310955 | solution.py:30
  285.9 79.1 %reduce-scatter.4.cloned.1.call-done = bf16[192,1024]{1,0:T(8,128)(2,1)} async-done(((bf16[6144,1024]{1,0:T(8,128)(2,1)}), bf16[192,1024]{1,0:T(8,128)(2,1)}) %reduce-scatter.4.cloned.1.call-update) | async-done | bytes 393232
  364.9 2.0 copy.83
  368.1 2.2 copy.75
  370.3 2.7 fusion.12
  373.0 2.0 copy.74
  375.0 32.9 %all-reduce.5.cloned.1.call-done = bf16[192,1024]{0,1:T(8,128)(2,1)} async-done(((bf16[192,1024]{0,1:T(8,128)(2,1)}), bf16[192,1024]{0,1:T(8,128)(2,1)}) %all-reduce.5.cloned.1.call-update) | async-done | bytes 393232 | tf_op jit(solution)/shard_map/psum | solution.py:182
  408.0 2.1 convert_multiply_fusion
  410.0 2.4 copy.76
  (148 shorter events, 56.9 us)
Async XLA Ops:
  7.2 165.6 %copy-start = (bf16[1,256,6144]{2,1,0:T(8,128)(2,1)S(1)}, bf16[1,256,6144]{2,1,0:T(8,128)(2,1)}, u32[]{:S(2)}) copy-start(bf16[1,256,6144]{2,1,0:T(8,128)(2,1)} %param.14) | copy-start | bytes 9437188
  7.2 17.1 %copy-start.20 = (u32[256]{0:T(256)S(1)}, u32[256]{0:T(256)}, u32[]{:S(2)}) copy-start(u32[256]{0:T(256)} %constant.96) | copy-start | bytes 3076
  7.2 13.4 %copy-start.19 = (f32[8]{0:T(128)S(1)}, f32[8]{0:T(128)}, u32[]{:S(2)}) copy-start(f32[8]{0:T(128)} %param.16) | copy-start | bytes 100
  7.2 91.6 %all-gather.10.cloned.1.call-start = ((), (), s32[]{:S(2)}) async-start(), calls=%async_computation.3 | async-start | bytes 8650752 | tf_op jit(solution)/shard_map/all_gather | solution.py:15
  23.5 132.6 %all-gather.8.cloned.1.call-start = ((), (), s32[]{:S(2)}) async-start(), calls=%async_computation.1 | async-start | bytes 12976128 | tf_op jit(solution)/shard_map/all_gather | solution.py:167
  24.2 226.6 %all-gather.12.cloned.1.call-start = ((), (), s32[]{:S(2)}) async-start(), calls=%async_computation.4 | async-start | bytes 8650752 | tf_op jit(solution)/shard_map/all_gather | solution.py:15
  94.2 3.1 copy-start.9
  96.3 1.0 copy-start.13
  172.8 7.0 %copy-start.12 = (f32[256,8,128]{0,2,1:T(8,128)S(1)}, f32[256,8,128]{0,2,1:T(8,128)}, u32[]{:S(2)}) copy-start(f32[256,8,128]{0,2,1:T(8,128)} %get-tuple-element.186) | copy-start | bytes 3145732
  179.8 1.9 copy-start.6
  182.7 182.2 %reduce-scatter.4.cloned.1.call-start = ((), (), s32[]{:S(2)}) async-start(), calls=%async_computation.5 | async-start | bytes 12976128
  206.9 1.0 copy-start.5
  206.9 1.2 copy-start.10
  206.9 1.9 copy-start.18
  207.0 201.0 %all-reduce.5.cloned.1.call-start = ((), (), s32[]{:S(2)}) async-start(), calls=%async_computation.2 | async-start | bytes 1048576 | tf_op jit(solution)/shard_map/psum | solution.py:182
  208.1 1.2 copy-start.3
  208.8 1.0 copy-start.16
  208.8 2.0 copy-start.14
  209.3 2.8 copy-start.7
  210.8 1.3 copy-start.17
  250.9 116.1 %copy-start.11 = (bf16[32,8,8,128]{3,2,1,0:T(8,128)(2,1)S(1)}, bf16[32,8,8,128]{3,2,1,0:T(8,128)(2,1)}, u32[]{:S(2)}) copy-start(bf16[32,8,8,128]{3,2,1,0:T(8,128)(2,1)} %copy.85) | copy-start | bytes 1572868
  250.9 116.1 %copy-start.15 = (f32[256,8,128]{0,2,1:T(8,128)S(1)}, f32[256,8,128]{0,2,1:T(8,128)}, u32[]{:S(2)}) copy-start(f32[256,8,128]{0,2,1:T(8,128)} %convolution_bitcast_fusion.5) | copy-start | bytes 3145732
  285.9 81.1 %copy-start.2 = (f32[8,128,128]{2,1,0:T(8,128)}, f32[8,128,128]{2,1,0:T(8,128)S(1)}, u32[]{:S(2)}) copy-start(f32[8,128,128]{2,1,0:T(8,128)S(1)} %get-tuple-element.133) | copy-start | bytes 1572868
  368.1 44.3 %copy-start.1 = (bf16[1,256,6144]{2,1,0:T(8,128)(2,1)S(1)}, bf16[1,256,6144]{2,1,0:T(8,128)(2,1)}, u32[]{:S(2)}) copy-start(bf16[1,256,6144]{2,1,0:T(8,128)(2,1)} %param.14) | copy-start | bytes 9437188
  (2 other events, 1.6 us)
Sparse Core Ops, SparseCore 0:
  23.6 62.5 all-gather.9
  88.7 67.3 all-gather.7
  182.9 67.9 all-gather.11
  254.8 110.0 reduce-scatter.3
  367.6 40.3 all-reduce.4
where the time goes:
time: 422 us; the launch traced here: 419 us
  waiting for transfers between devices  201 us (48%)
  blocking collectives  66.1 us (16%)
  local copies, waits for them, and re-layouts  59 us (14%)
  other arithmetic  42.3 us (10%)
  matrix products  31.7 us (8%)
  between operations  17.3 us (4%)
    unnamed x6, waiting for transfers between devices  79.8 us
    unnamed x1, blocking collectives  66.1 us
    all_gather x1, waiting for transfers between devices, local(): lax.all_gather(out_weight, 'seq', axis=0, tiled=True)  51.4 us
    all_gather x2, waiting for transfers between devices, prefix(): lax.all_gather(a.astype(kind), axis)  37.4 us
    add x31, other arithmetic, combine_states(): later[0][:, None, None] * earlier[1] + later[1]  35.8 us
    unnamed x55, local copies, waits for them, and re-layouts  34.2 us
    psum x1, waiting for transfers between devices, local(): grad_weight = lax.psum(weight_part, 'dp').astype(jnp.float32) * norm_factor  32.9 us
    dot_general x1, local copies, waits for them, and re-layouts, local(): jnp.dot(columns, lax.all_gather(out_weight, 'seq', axis=0, tiled=True), p...  16.7 us
  transfers between devices with their start and end apart: 5, of which 4 were waited for; matrix products, arithmetic and copies ran while one was open for 20% of the time, Pallas kernels for 0%

commit v1 on v0

--- a/solution.py
+++ b/solution.py
@@ -179,7 +179,12 @@
         tiled=True,
     )
     norm_factor = (lax.axis_size("dp") * seq_count * tok_count) ** (-0.5)
-    grad_weight = lax.psum(weight_part, "dp").astype(jnp.float32) * norm_factor
+
+    def tails_arrange(array_in):
+        a_next = jnp.sum(jax.lax.all_gather(array_in, "dp"), 0)
+        return a_next
+
+    grad_weight = tails_arrange(weight_part).astype(jnp.float32) * norm_factor
     grad_attn, grad_scores, back_local = backward_local(
         queries,
         values_here,

time: 422 us -> 389 us (0.922)
  waiting for transfers between devices: 201 us -> 160 us
  blocking collectives: 66.1 us -> 77.4 us
    unnamed x6 -> x4, waiting for transfers between devices: 79.8 us -> 0.74 us
    reduce_scatter x0 -> x1, waiting for transfers between devices: none -> 70 us  [local(): lax.psum_scatter(part.astype(jnp.bfloat16).astype(jnp.float32).astype(jnp...]
    psum x1 -> x0, waiting for transfers between devices: 32.9 us -> none  [local(): grad_weight = lax.psum(weight_part, 'dp').astype(jnp.float32) * norm_factor]
    all_gather x0 -> x1, blocking collectives: none -> 11.6 us  [tails_arrange(): a_next = jnp.sum(jax.lax.all_gather(array_in, 'dp'), 0)]
    unnamed x55 -> x53, local copies, waits for them, and re-layouts: 34.2 us -> 30.7 us
  transfers between devices with their start and end apart: 5 -> 4, of which waited for: 4 -> 3; matrix products, arithmetic and copies ran while one was open for 20% -> 22% of each run, Pallas kernels for 0% -> 0%
where the time goes in v1:
time: 389 us; the launch traced here: 386 us
  waiting for transfers between devices  160 us (41%)
  blocking collectives  77.4 us (20%)
  local copies, waits for them, and re-layouts  55.6 us (14%)
  other arithmetic  42.5 us (11%)
  matrix products  31.9 us (8%)
  between operations  17.3 us (4%)
    reduce_scatter x1, waiting for transfers between devices, local(): lax.psum_scatter(part.astype(jnp.bfloat16).astype(jnp.float32).astype(jnp...  70 us
    unnamed x1, blocking collectives  65.7 us
    all_gather x1, waiting for transfers between devices, local(): lax.all_gather(out_weight, 'seq', axis=0, tiled=True)  51.6 us
    all_gather x2, waiting for transfers between devices, prefix(): lax.all_gather(a.astype(kind), axis)  37.3 us
    add x31, other arithmetic, combine_states(): later[0][:, None, None] * earlier[1] + later[1]  35.8 us
    unnamed x53, local copies, waits for them, and re-layouts  30.7 us
    dot_general x1, local copies, waits for them, and re-layouts, local(): jnp.dot(columns, lax.all_gather(out_weight, 'seq', axis=0, tiled=True), p...  16.8 us
    all_gather x1, blocking collectives, tails_arrange(): a_next = jnp.sum(jax.lax.all_gather(array_in, 'dp'), 0)  11.6 us
  transfers between devices with their start and end apart: 4, of which 3 were waited for; matrix products, arithmetic and copies ran while one was open for 22% of the time, Pallas kernels for 0%

profile of v1, /device:TPU:1, one launch (start us, length us, event | category | flops | bytes accessed | tf_op | source)
XLA Modules:
  0.0 385.5 jit_solution(10837680581630956489)
XLA Ops:
  12.7 2.7 bitcast_compare_fusion.3
  15.4 1.9 copy.84
  17.3 2.1 copy.57
  21.4 2.0 convolution_convert_fusion.1
  26.0 65.7 %all-reduce.2 = (bf16[256]{0:T(256)(128)(2,1)S(1)}, bf16[256]{0:T(256)(128)(2,1)S(1)}) all-reduce(bf16[256]{0:T(256)(128)(2,1)S(1)} %dynamic-update-slice, bf16[256]{0:T(256)(128)(2,1)S(1)} %dynamic-update-slice.1), channel_id=2, replica_groups=mesh['dp'=2,'seq'=32,'head'=4] {'seq'}, use_global_device_ids=true, to_apply=%add | all-reduce | flops 512 | bytes 2048
  91.9 2.1 copy.83
  94.2 1.9 multiply_convert_fusion.1
  97.0 1.5 convolution_bitcast_fusion.7
  99.4 2.1 while.26
  99.4 2.1 convert_add_fusion.4
  101.5 3.0 multiply_reduce_fusion.1
  104.5 51.6 %all-gather.9.cloned.1.call-done = bf16[6144,1024]{1,0:T(8,128)(2,1)} async-done(((bf16[192,1024]{1,0:T(8,128)(2,1)}), bf16[6144,1024]{1,0:T(8,128)(2,1)}) %all-gather.9.cloned.1.call-update) | async-done | bytes 12582928 | tf_op jit(solution)/shard_map/all_gather | solution.py:167
  156.1 16.8 %copy.61 = bf16[1024,6144]{1,0:T(8,128)(2,1)} copy(bf16[1024,6144]{0,1:T(8,128)(2,1)} %bitcast.112) | data formatting | bytes 25165824 | tf_op jit(solution)/shard_map/dot_general | solution.py:165
  172.9 7.0 %multiply_reduce_fusion = (f32[256,8]{0,1:T(8,128)S(1)}, f32[256,8,128]{0,2,1:T(8,128)S(1)}) fusion(f32[256,8,128]{0,2,1:T(8,128)} %get-tuple-element.186, f32[256,8]{0,1:T(8,128)S(1)} %add_rsqrt_fusion, bf16[8,128,6144]{2,1,0:T(8,128)(2,1)} %bitcast.113, bf16[1,256,6144]{2,1,0:T(8,128)(2,1)S(1)} %copy-done), kind=kOutput, calls=%fused_computation.34 | convolution fusion | flops 3222009856 | bytes 17842176 | tf_op jit(solution)/shard_map/dot_general | solution.py:165
  182.9 7.5 %convert_bitcast_fusion = bf16[6144,1024]{0,1:T(8,128)(2,1)} fusion(bf16[256,1024]{0,1:T(8,128)(2,1)} %bitcast.129, bf16[1,256,6144]{2,1,0:T(8,128)(2,1)S(1)} %copy-done), kind=kOutput, calls=%fused_computation.4 | convolution fusion | flops 3227516928 | bytes 16252928 | tf_op jit(solution)/shard_map/dot_general | solution.py:172
  190.4 16.7 %copy.81 = bf16[6144,1024]{1,0:T(8,128)(2,1)} copy(bf16[6144,1024]{0,1:T(8,128)(2,1)} %convert_bitcast_fusion) | data formatting | bytes 25165824
  212.3 1.3 convolution_bitcast_fusion.4
  213.6 37.3 %all-gather.13.cloned.1.call-done = bf16[256,128,128]{2,1,0:T(8,128)(2,1)} async-done(((bf16[8,128,128]{2,1,0:T(8,128)(2,1)}), bf16[256,128,128]{2,1,0:T(8,128)(2,1)}) %all-gather.13.cloned.1.call-update) | async-done | bytes 8388624 | tf_op jit(solution)/shard_map/all_gather | solution.py:15
  251.0 35.0 %while.27 = (s32[]{:T(128)}, f32[8,128,128]{2,1,0:T(8,128)S(1)}, s32[]{:T(128)}, bf16[32,8]{1,0:T(8,128)(2,1)S(1)}, bf16[32,8,128,128]{3,2,1,0:T(8,128)(2,1)}, /*index=5*/s32[]{:T(128)}, s32[]{:T(128)}, s32[]{:T(128)}, s32[]{:T(128)}) while((s32[]{:T(128)}, f32[8,128,128]{2,1,0:T(8,128)S(1)}, s32[]{:T(128)}, bf16[32,8]{1,0:T(8,128)(2,1)S(1)}, ...), condition=%wide.region_5.6_spmd, body=%wide.region_4.5_spmd.sunk | while | flops 393230 | bytes 1310955 | solution.py:30
  288.0 2.2 copy.75
  290.2 2.8 fusion.12
  293.0 2.1 copy.74
  295.1 70.0 %reduce-scatter.4.cloned.1.call-done = bf16[192,1024]{1,0:T(8,128)(2,1)} async-done(((bf16[6144,1024]{1,0:T(8,128)(2,1)}), bf16[192,1024]{1,0:T(8,128)(2,1)}) %reduce-scatter.4.cloned.1.call-update) | async-done | bytes 393232 | tf_op jit(solution)/shard_map/reduce_scatter | solution.py:175
  365.1 11.6 %all-gather.4 = bf16[384,1024]{1,0:T(8,128)(2,1)} all-gather(bf16[192,1024]{1,0:T(8,128)(2,1)} %reduce-scatter.4.cloned.1.call-done), channel_id=6, replica_groups=mesh['dp'=2,'seq'=32,'head'=4] {'dp'}, dimensions={0}, use_global_device_ids=true | all-gather | bytes 1179648 | tf_op jit(solution)/shard_map/all_gather | solution.py:184
  (145 shorter events, 55.3 us)
Async XLA Ops:
  7.2 165.7 %copy-start = (bf16[1,256,6144]{2,1,0:T(8,128)(2,1)S(1)}, bf16[1,256,6144]{2,1,0:T(8,128)(2,1)}, u32[]{:S(2)}) copy-start(bf16[1,256,6144]{2,1,0:T(8,128)(2,1)} %param.14) | copy-start | bytes 9437188
  7.2 17.1 %copy-start.20 = (u32[256]{0:T(256)S(1)}, u32[256]{0:T(256)}, u32[]{:S(2)}) copy-start(u32[256]{0:T(256)} %constant.98) | copy-start | bytes 3076
  7.2 13.4 %copy-start.19 = (f32[8]{0:T(128)S(1)}, f32[8]{0:T(128)}, u32[]{:S(2)}) copy-start(f32[8]{0:T(128)} %param.16) | copy-start | bytes 100
  7.2 91.4 %all-gather.11.cloned.1.call-start = ((), (), s32[]{:S(2)}) async-start(), calls=%async_computation.2 | async-start | bytes 8650752 | tf_op jit(solution)/shard_map/all_gather | solution.py:15
  23.5 132.6 %all-gather.9.cloned.1.call-start = ((), (), s32[]{:S(2)}) async-start(), calls=%async_computation.1 | async-start | bytes 12976128 | tf_op jit(solution)/shard_map/all_gather | solution.py:167
  24.2 226.7 %all-gather.13.cloned.1.call-start = ((), (), s32[]{:S(2)}) async-start(), calls=%async_computation.3 | async-start | bytes 8650752 | tf_op jit(solution)/shard_map/all_gather | solution.py:15
  93.9 3.1 copy-start.9
  96.1 1.0 copy-start.13
  172.9 7.0 %copy-start.12 = (f32[256,8,128]{0,2,1:T(8,128)S(1)}, f32[256,8,128]{0,2,1:T(8,128)}, u32[]{:S(2)}) copy-start(f32[256,8,128]{0,2,1:T(8,128)} %get-tuple-element.186) | copy-start | bytes 3145732
  179.9 1.9 copy-start.6
  181.0 0.8 copy-start.4
  182.9 182.2 %reduce-scatter.4.cloned.1.call-start = ((), (), s32[]{:S(2)}) async-start(), calls=%async_computation.4 | async-start | bytes 12976128 | tf_op jit(solution)/shard_map/reduce_scatter | solution.py:175
  207.1 1.0 copy-start.5
  207.1 1.2 copy-start.10
  207.1 1.9 copy-start.18
  208.3 1.2 copy-start.3
  209.0 1.0 copy-start.16
  209.0 2.0 copy-start.14
  209.5 2.8 copy-start.7
  211.0 1.3 copy-start.17
  251.0 35.8 %copy-start.15 = (f32[256,8,128]{0,2,1:T(8,128)S(1)}, f32[256,8,128]{0,2,1:T(8,128)}, u32[]{:S(2)}) copy-start(f32[256,8,128]{0,2,1:T(8,128)} %convolution_bitcast_fusion.5) | copy-start | bytes 3145732
  251.0 35.8 %copy-start.11 = (bf16[32,8,8,128]{3,2,1,0:T(8,128)(2,1)S(1)}, bf16[32,8,8,128]{3,2,1,0:T(8,128)(2,1)}, u32[]{:S(2)}) copy-start(bf16[32,8,8,128]{3,2,1,0:T(8,128)(2,1)} %copy.84) | copy-start | bytes 1572868
  286.0 0.8 copy-start.2
  288.0 91.0 %copy-start.1 = (bf16[1,256,6144]{2,1,0:T(8,128)(2,1)S(1)}, bf16[1,256,6144]{2,1,0:T(8,128)(2,1)}, u32[]{:S(2)}) copy-start(bf16[1,256,6144]{2,1,0:T(8,128)(2,1)} %param.14) | copy-start | bytes 9437188
  (1 other events, 0.8 us)
Sparse Core Ops, SparseCore 0:
  23.6 62.4 all-gather.10
  88.7 67.3 all-gather.8
  183.0 67.9 all-gather.12
  255.0 110.0 reduce-scatter.3
